TPU v7x, 256 devices: a whole 4x4x8 slice. The times are simulated.
256 devices in a mesh: gx: 8 (over x, core), gy: 32 (over y, z).
Axes of the slice: x: 4, y: 4, z: 8, core: 2. Of those that a mesh axis runs over, the one named last changes fastest.
Arguments:
- fields: bfloat16 [672, 672, 1536], P('gx', 'gy'), may hold values from -16 to 16
- x_factor: bfloat16 [672, 336], replicated, may hold values from -0.00030517578 to 0.00030517578
- running_r: float32 [672, 672], replicated, as said below
Outputs:
- new_r: float32 [672, 672], P('gy', 'gx')
Inputs may be any that keep to these rules, and one draw needn't show every extreme that they name: `running_r`: upper triangular with a positive diagonal.
All inputs are finite; a program needn't handle non-finite values.
Results may differ from a plain program's by a relative error of at most 0.0003.
Values may be sent and summed in bfloat16 or wider, within the bound.
A program may use at most 256 MiB of HBM per device.

v0:
```python
import jax
import jax.numpy as jnp
from jax import lax
from jax.sharding import PartitionSpec as P


def fibre_gram(fibres):
    local_gram = lax.dot_general(
        fibres, fibres, (((0, 2), (0, 2)), ((), ())), preferred_element_type=jnp.float32
    )
    return lax.psum(local_gram, ("gx", "gy"))


def project_local(x_factor, block):
    full_x = block.shape[0]
    middle = block.shape[1]
    part_cells = block.shape[2]
    product = lax.dot_general(
        x_factor,
        block.reshape(full_x, middle * part_cells),
        (((0,), (0,)), ((), ())),
        preferred_element_type=jnp.float32,
    )
    return product.astype(jnp.bfloat16).reshape(x_factor.shape[1], middle, part_cells)


def on_device(fields, x_factor, running_r):
    full_y = running_r.shape[0]
    exchanged = lax.all_to_all(fields, "gx", split_axis=2, concat_axis=0, tiled=True)
    projected = project_local(x_factor, exchanged)
    fibres = lax.all_to_all(projected, "gy", split_axis=2, concat_axis=1, tiled=True)
    gram_sum = fibre_gram(fibres)
    total = (
        jnp.dot(
            running_r.T,
            running_r,
            precision=lax.Precision.HIGHEST,
            preferred_element_type=jnp.float32,
        )
        + gram_sum
    )
    upper_r = jnp.linalg.cholesky(total).T
    row_block = full_y // lax.axis_size("gy")
    col_block = full_y // lax.axis_size("gx")
    return lax.dynamic_slice(
        upper_r,
        (lax.axis_index("gy") * row_block, lax.axis_index("gx") * col_block),
        (row_block, col_block),
    )


def solution(mesh):
    in_specs = (P("gx", "gy", None), P(), P())
    out_specs = P("gy", "gx")
    return jax.shard_map(
        on_device, mesh=mesh, in_specs=in_specs, out_specs=out_specs, check_vma=False
    )
```

profile of v0, /device:TPU:2, one launch (start us, length us, event | category | flops | bytes accessed | tf_op | source)
XLA Modules:
  0.0 698.8 jit_solution(13633956588699801760)
XLA Ops:
  6.5 11.8 %copy.19 = bf16[84,21,1536]{0,1,2:T(8,128)(2,1)} copy(bf16[84,21,1536]{2,0,1:T(8,128)(2,1)} %param.3) | data formatting | bytes 10838016 | tf_op args[0]
  18.4 114.1 %all_to_all.33 = bf16[84,21,1536]{0,1,2:T(8,128)(2,1)} all-to-all(bf16[84,21,1536]{0,1,2:T(8,128)(2,1)} %copy.19), channel_id=1, replica_groups=mesh['gx'=8,'gy'=32] {'gx'}, dimensions={2} | all-to-all | bytes 10838016 | tf_op jit(solution)/shard_map/all_to_all | solution.py:29
  132.5 15.4 %copy.20 = bf16[84,21,8,192]{3,1,0,2:T(8,128)(2,1)} copy(bf16[84,21,8,192]{0,1,3,2:T(8,128)(2,1)} %bitcast.50) | data formatting | bytes 10838016 | tf_op jit(solution)/shard_map/all_to_all | solution.py:29
  147.9 12.5 %reshape.46 = bf16[672,4032]{1,0:T(8,128)(2,1)} reshape(bf16[8,84,21,192]{3,2,1,0:T(8,128)(2,1)} %bitcast.51) | data formatting | bytes 10838016 | tf_op jit(solution)/shard_map/reshape | solution.py:20
  160.4 6.4 convolution_convert_fusion
  166.8 4.5 copy.21
  171.3 3.7 copy.22
  175.1 91.4 %all_to_all.34 = bf16[336,21,192]{0,1,2:T(8,128)(2,1)S(1)} all-to-all(bf16[336,21,192]{0,1,2:T(8,128)(2,1)S(1)} %copy.22), channel_id=1, replica_groups=mesh['gx'=8,'gy'=32] {'gy'}, dimensions={2} | all-to-all | bytes 5419008 | tf_op jit(solution)/shard_map/all_to_all | solution.py:31
  266.5 2.2 copy.23
  268.7 6.0 all_to_all.30
  274.7 6.8 convolution_bitcast_fusion
  281.5 257.3 %all-reduce.3.cloned.1.call-done = f32[672,672]{0,1:T(8,128)} async-done(((f32[672,672]{0,1:T(8,128)}), f32[672,672]{0,1:T(8,128)}) %all-reduce.3.cloned.1.call-update) | async-done | bytes 1806352 | tf_op jit(solution)/shard_map/psum | solution.py:11
  538.8 8.2 %convolution_add_fusion = f32[672,672]{0,1:T(8,128)} fusion(f32[672,672]{0,1:T(8,128)} %all-reduce.3.cloned.1.call-done, f32[672,672]{1,0:T(8,128)S(1)} %copy-done), kind=kOutput, calls=%fused_computation.4 | convolution fusion | flops 3642024960 | bytes 5419008 | tf_op jit(solution)/shard_map/dot_general | solution.py:34
  547.0 3.1 copy.27
  550.2 2.5 fusion
  554.0 11.7 %cholesky.166 = f32[128,128]{1,0:T(8,128)S(1)} custom-call(f32[128,128]{1,0:T(8,128)S(1)} %cholesky.430), custom_call_target="Cholesky" | custom-call | tf_op jit(solution)/shard_map/jit(cholesky)/cholesky | solution.py:42
  565.7 9.8 %custom-call.43 = f32[1,128,128]{1,2,0:T(8,128)S(1)} custom-call(f32[1,128,128]{2,1,0:T(8,128)S(1)} %get-tuple-element.18), custom_call_target="InvertDiagBlocksLowerTriangular" | custom-call | tf_op jit(solution)/shard_map/jit(cholesky)/cholesky | solution.py:42
  575.6 1.4 cholesky.342
  577.0 2.1 constant_dynamic-update-slice_fusion.4
  579.0 1.3 convolution_subtract_fusion
  580.4 11.7 %cholesky.189 = f32[128,128]{1,0:T(8,128)S(1)} custom-call(f32[128,128]{1,0:T(8,128)S(1)} %cholesky.434), custom_call_target="Cholesky" | custom-call | tf_op jit(solution)/shard_map/jit(cholesky)/cholesky | solution.py:42
  592.8 10.2 %custom-call.44 = f32[1,128,128]{1,2,0:T(8,128)S(1)} custom-call(f32[1,128,128]{2,1,0:T(8,128)S(1)} %get-tuple-element.15), custom_call_target="InvertDiagBlocksLowerTriangular" | custom-call | tf_op jit(solution)/shard_map/jit(cholesky)/cholesky | solution.py:42
  604.0 1.6 convolution_subtract_fusion.1
  605.6 11.7 %cholesky.356 = f32[128,128]{1,0:T(8,128)S(1)} custom-call(f32[128,128]{1,0:T(8,128)S(1)} %cholesky.439), custom_call_target="Cholesky" | custom-call | tf_op jit(solution)/shard_map/jit(cholesky)/cholesky | solution.py:42
  618.7 9.8 %custom-call.45 = f32[1,128,128]{1,2,0:T(8,128)S(1)} custom-call(f32[1,128,128]{2,1,0:T(8,128)S(1)} %get-tuple-element.12), custom_call_target="InvertDiagBlocksLowerTriangular" | custom-call | tf_op jit(solution)/shard_map/jit(cholesky)/cholesky | solution.py:42
  629.4 1.7 convolution_subtract_fusion.2
  631.1 11.8 %cholesky.375 = f32[128,128]{1,0:T(8,128)S(1)} custom-call(f32[128,128]{1,0:T(8,128)S(1)} %cholesky.444), custom_call_target="Cholesky" | custom-call | tf_op jit(solution)/shard_map/jit(cholesky)/cholesky | solution.py:42
  644.3 9.8 %custom-call.46 = f32[1,128,128]{1,2,0:T(8,128)S(1)} custom-call(f32[1,128,128]{2,1,0:T(8,128)S(1)} %get-tuple-element.9), custom_call_target="InvertDiagBlocksLowerTriangular" | custom-call | tf_op jit(solution)/shard_map/jit(cholesky)/cholesky | solution.py:42
  655.0 1.5 convolution_subtract_fusion.3
  656.5 11.7 %cholesky.394 = f32[128,128]{1,0:T(8,128)S(1)} custom-call(f32[128,128]{1,0:T(8,128)S(1)} %cholesky.449), custom_call_target="Cholesky" | custom-call | tf_op jit(solution)/shard_map/jit(cholesky)/cholesky | solution.py:42
  669.5 9.8 %custom-call.47 = f32[1,128,128]{1,2,0:T(8,128)S(1)} custom-call(f32[1,128,128]{2,1,0:T(8,128)S(1)} %get-tuple-element.6), custom_call_target="InvertDiagBlocksLowerTriangular" | custom-call | tf_op jit(solution)/shard_map/jit(cholesky)/cholesky | solution.py:42
  681.3 2.9 cholesky.415
  (31 shorter events, 14.5 us)
Async XLA Ops:
  6.5 532.3 %copy-start = (f32[672,672]{1,0:T(8,128)S(1)}, f32[672,672]{1,0:T(8,128)}, u32[]{:S(2)}) copy-start(f32[672,672]{1,0:T(8,128)} %param.5) | copy-start | bytes 5419012
  6.5 532.3 %all-reduce.3.cloned.1.call-start = ((), (), s32[]{:S(2)}) async-start(), calls=%async_computation.2 | async-start | bytes 4128768 | tf_op jit(solution)/shard_map/psum | solution.py:11
  147.9 12.5 %copy-start.2 = (bf16[672,336]{1,0:T(8,128)(2,1)S(1)}, bf16[672,336]{1,0:T(8,128)(2,1)}, u32[]{:S(2)}) copy-start(bf16[672,336]{1,0:T(8,128)(2,1)} %param.4) | copy-start | bytes 1354756
  552.6 1.3 copy-start.1
Sparse Core Ops, SparseCore 0:
  281.6 257.1 all-reduce.2
where the time goes:
time: 706 us; the launch traced here: 699 us
  waiting for transfers between devices  257 us (36%)
  blocking collectives  206 us (29%)
  other arithmetic  121 us (17%)
  local copies, waits for them, and re-layouts  62.8 us (9%)
  matrix products  34.5 us (5%)
  between operations  17.6 us (2%)
    psum x1, waiting for transfers between devices, fibre_gram(): return lax.psum(local_gram, ('gx', 'gy'))  257 us
    another operation x22, other arithmetic, on_device(): upper_r = jnp.linalg.cholesky(total).T  118 us
    all_to_all x1, blocking collectives, on_device(): lax.all_to_all(fields, 'gx', split_axis=2, concat_axis=0, tiled=True)  114 us
    all_to_all x1, blocking collectives, on_device(): lax.all_to_all(projected, 'gy', split_axis=2, concat_axis=1, tiled=True)  91.4 us
    all_to_all x1, local copies, waits for them, and re-layouts, on_device(): lax.all_to_all(fields, 'gx', split_axis=2, concat_axis=0, tiled=True)  15.4 us
  transfers between devices with their start and end apart: 1, of which 1 were waited for; matrix products, arithmetic and copies ran while one was open for 0% of the time, Pallas kernels for 0%

commit v1 on v0

--- a/solution.py
+++ b/solution.py
@@ -4,11 +4,16 @@
 from jax.sharding import PartitionSpec as P
 
 
+def by_each_axis(value, axis_one, axis_two):
+    inner = lax.psum(value, axis_one)
+    return lax.psum(inner, axis_two)
+
+
 def fibre_gram(fibres):
     local_gram = lax.dot_general(
         fibres, fibres, (((0, 2), (0, 2)), ((), ())), preferred_element_type=jnp.float32
     )
-    return lax.psum(local_gram, ("gx", "gy"))
+    return by_each_axis(local_gram, "gx", "gy")
 
 
 def project_local(x_factor, block):

time: 706 us -> 672 us (0.952)
  waiting for transfers between devices: 257 us -> 222 us
    psum x1 -> x2, waiting for transfers between devices: 257 us -> 222 us  [the longest x1 159 us: by_each_axis(): return lax.psum(inner, axis_two)]
  transfers between devices with their start and end apart: 1 -> 2, of which waited for: 1 -> 2; matrix products, arithmetic and copies ran while one was open for 0% -> 0% of each run, Pallas kernels for 0% -> 0%
where the time goes in v1:
time: 672 us; the launch traced here: 664 us
  waiting for transfers between devices  222 us (33%)
  blocking collectives  205 us (31%)
  other arithmetic  121 us (18%)
  local copies, waits for them, and re-layouts  62.7 us (9%)
  matrix products  34.5 us (5%)
  between operations  17.6 us (3%)
    psum x1, waiting for transfers between devices, by_each_axis(): return lax.psum(inner, axis_two)  159 us
    another operation x22, other arithmetic, on_device(): upper_r = jnp.linalg.cholesky(total).T  118 us
    all_to_all x1, blocking collectives, on_device(): lax.all_to_all(fields, 'gx', split_axis=2, concat_axis=0, tiled=True)  114 us
    all_to_all x1, blocking collectives, on_device(): lax.all_to_all(projected, 'gy', split_axis=2, concat_axis=1, tiled=True)  91.2 us
    psum x1, waiting for transfers between devices, by_each_axis(): inner = lax.psum(value, axis_one)  63.8 us
    all_to_all x1, local copies, waits for them, and re-layouts, on_device(): lax.all_to_all(fields, 'gx', split_axis=2, concat_axis=0, tiled=True)  15.4 us
  transfers between devices with their start and end apart: 2, of which 2 were waited for; matrix products, arithmetic and copies ran while one was open for 0% of the time, Pallas kernels for 0%

profile of v1, /device:TPU:2, one launch (start us, length us, event | category | flops | bytes accessed | tf_op | source)
XLA Modules:
  0.0 664.0 jit_solution(2034544013017403192)
XLA Ops:
  6.5 11.8 %copy.19 = bf16[84,21,1536]{0,1,2:T(8,128)(2,1)} copy(bf16[84,21,1536]{2,0,1:T(8,128)(2,1)} %param.3) | data formatting | bytes 10838016 | tf_op args[0]
  18.4 114.1 %all_to_all.33 = bf16[84,21,1536]{0,1,2:T(8,128)(2,1)} all-to-all(bf16[84,21,1536]{0,1,2:T(8,128)(2,1)} %copy.19), channel_id=1, replica_groups=mesh['gx'=8,'gy'=32] {'gx'}, dimensions={2} | all-to-all | bytes 10838016 | tf_op jit(solution)/shard_map/all_to_all | solution.py:34
  132.5 15.4 %copy.20 = bf16[84,21,8,192]{3,1,0,2:T(8,128)(2,1)} copy(bf16[84,21,8,192]{0,1,3,2:T(8,128)(2,1)} %bitcast.50) | data formatting | bytes 10838016 | tf_op jit(solution)/shard_map/all_to_all | solution.py:34
  147.9 12.5 %reshape.46 = bf16[672,4032]{1,0:T(8,128)(2,1)} reshape(bf16[8,84,21,192]{3,2,1,0:T(8,128)(2,1)} %bitcast.51) | data formatting | bytes 10838016 | tf_op jit(solution)/shard_map/reshape | solution.py:25
  160.4 6.4 convolution_convert_fusion
  166.8 4.5 copy.21
  171.3 3.7 copy.22
  175.1 91.2 %all_to_all.34 = bf16[336,21,192]{0,1,2:T(8,128)(2,1)S(1)} all-to-all(bf16[336,21,192]{0,1,2:T(8,128)(2,1)S(1)} %copy.22), channel_id=1, replica_groups=mesh['gx'=8,'gy'=32] {'gy'}, dimensions={2} | all-to-all | bytes 5419008 | tf_op jit(solution)/shard_map/all_to_all | solution.py:36
  266.3 2.2 copy.23
  268.5 6.0 all_to_all.30
  274.5 6.8 %convolution_bitcast_fusion = f32[672,672]{0,1:T(8,128)} fusion(bf16[336,672,6]{0,1,2:T(8,128)(2,1)} %all_to_all.30), kind=kOutput, calls=%fused_computation.3 | convolution fusion | flops 1820786688 | bytes 4515840 | tf_op jit(solution)/shard_map/dot_general | solution.py:13
  281.6 63.8 %all-reduce.4.cloned.1.call-done = f32[672,672]{0,1:T(8,128)} async-done(((f32[672,672]{0,1:T(8,128)}), f32[672,672]{0,1:T(8,128)}) %all-reduce.4.cloned.1.call-update) | async-done | bytes 1806352 | tf_op jit(solution)/shard_map/psum | solution.py:8
  345.4 158.6 %all-reduce.6.cloned.1.call-done = f32[672,672]{0,1:T(8,128)} async-done(((f32[672,672]{0,1:T(8,128)}), f32[672,672]{0,1:T(8,128)}) %all-reduce.6.cloned.1.call-update) | async-done | bytes 1806352 | tf_op jit(solution)/shard_map/psum | solution.py:9
  504.0 8.3 %convolution_add_fusion = f32[672,672]{0,1:T(8,128)} fusion(f32[672,672]{0,1:T(8,128)} %all-reduce.6.cloned.1.call-done, f32[672,672]{1,0:T(8,128)S(1)} %copy-done), kind=kOutput, calls=%fused_computation.4 | convolution fusion | flops 3642024960 | bytes 5419008 | tf_op jit(solution)/shard_map/dot_general | solution.py:39
  512.3 3.1 copy.27
  515.4 2.5 fusion
  519.2 11.7 %cholesky.166 = f32[128,128]{1,0:T(8,128)S(1)} custom-call(f32[128,128]{1,0:T(8,128)S(1)} %cholesky.430), custom_call_target="Cholesky" | custom-call | tf_op jit(solution)/shard_map/jit(cholesky)/cholesky | solution.py:47
  531.0 9.8 %custom-call.43 = f32[1,128,128]{1,2,0:T(8,128)S(1)} custom-call(f32[1,128,128]{2,1,0:T(8,128)S(1)} %get-tuple-element.18), custom_call_target="InvertDiagBlocksLowerTriangular" | custom-call | tf_op jit(solution)/shard_map/jit(cholesky)/cholesky | solution.py:47
  540.8 1.4 cholesky.342
  542.2 2.1 constant_dynamic-update-slice_fusion.4
  545.6 11.7 %cholesky.189 = f32[128,128]{1,0:T(8,128)S(1)} custom-call(f32[128,128]{1,0:T(8,128)S(1)} %cholesky.434), custom_call_target="Cholesky" | custom-call | tf_op jit(solution)/shard_map/jit(cholesky)/cholesky | solution.py:47
  558.0 10.2 %custom-call.44 = f32[1,128,128]{1,2,0:T(8,128)S(1)} custom-call(f32[1,128,128]{2,1,0:T(8,128)S(1)} %get-tuple-element.15), custom_call_target="InvertDiagBlocksLowerTriangular" | custom-call | tf_op jit(solution)/shard_map/jit(cholesky)/cholesky | solution.py:47
  569.2 1.6 convolution_subtract_fusion.1
  570.9 11.7 %cholesky.356 = f32[128,128]{1,0:T(8,128)S(1)} custom-call(f32[128,128]{1,0:T(8,128)S(1)} %cholesky.439), custom_call_target="Cholesky" | custom-call | tf_op jit(solution)/shard_map/jit(cholesky)/cholesky | solution.py:47
  583.9 9.8 %custom-call.45 = f32[1,128,128]{1,2,0:T(8,128)S(1)} custom-call(f32[1,128,128]{2,1,0:T(8,128)S(1)} %get-tuple-element.12), custom_call_target="InvertDiagBlocksLowerTriangular" | custom-call | tf_op jit(solution)/shard_map/jit(cholesky)/cholesky | solution.py:47
  594.7 1.7 convolution_subtract_fusion.2
  596.3 11.8 %cholesky.375 = f32[128,128]{1,0:T(8,128)S(1)} custom-call(f32[128,128]{1,0:T(8,128)S(1)} %cholesky.444), custom_call_target="Cholesky" | custom-call | tf_op jit(solution)/shard_map/jit(cholesky)/cholesky | solution.py:47
  609.6 9.8 %custom-call.46 = f32[1,128,128]{1,2,0:T(8,128)S(1)} custom-call(f32[1,128,128]{2,1,0:T(8,128)S(1)} %get-tuple-element.9), custom_call_target="InvertDiagBlocksLowerTriangular" | custom-call | tf_op jit(solution)/shard_map/jit(cholesky)/cholesky | solution.py:47
  620.2 1.5 convolution_subtract_fusion.3
  621.7 11.7 %cholesky.394 = f32[128,128]{1,0:T(8,128)S(1)} custom-call(f32[128,128]{1,0:T(8,128)S(1)} %cholesky.449), custom_call_target="Cholesky" | custom-call | tf_op jit(solution)/shard_map/jit(cholesky)/cholesky | solution.py:47
  634.8 9.8 %custom-call.47 = f32[1,128,128]{1,2,0:T(8,128)S(1)} custom-call(f32[1,128,128]{2,1,0:T(8,128)S(1)} %get-tuple-element.6), custom_call_target="InvertDiagBlocksLowerTriangular" | custom-call | tf_op jit(solution)/shard_map/jit(cholesky)/cholesky | solution.py:47
  646.5 2.9 cholesky.415
  (34 shorter events, 16.1 us)
Async XLA Ops:
  6.5 497.5 %copy-start = (f32[672,672]{1,0:T(8,128)S(1)}, f32[672,672]{1,0:T(8,128)}, u32[]{:S(2)}) copy-start(f32[672,672]{1,0:T(8,128)} %param.5) | copy-start | bytes 5419012
  6.5 338.9 %all-reduce.4.cloned.1.call-start = ((), (), s32[]{:S(2)}) async-start(), calls=%async_computation.2 | async-start | bytes 4128768 | tf_op jit(solution)/shard_map/psum | solution.py:8
  147.9 12.5 %copy-start.2 = (bf16[672,336]{1,0:T(8,128)(2,1)S(1)}, bf16[672,336]{1,0:T(8,128)(2,1)}, u32[]{:S(2)}) copy-start(bf16[672,336]{1,0:T(8,128)(2,1)} %param.4) | copy-start | bytes 1354756
  281.3 222.7 %all-reduce.6.cloned.1.call-start = ((), (), s32[]{:S(2)}) async-start(), calls=%async_computation.3 | async-start | bytes 4128768 | tf_op jit(solution)/shard_map/psum | solution.py:9
  517.9 1.3 copy-start.1
Sparse Core Ops, SparseCore 0:
  281.5 63.9 all-reduce.3
  348.9 155.1 all-reduce.5

commit v2 on v0

--- a/solution.py
+++ b/solution.py
@@ -2,6 +2,12 @@
 import jax.numpy as jnp
 from jax import lax
 from jax.sharding import PartitionSpec as P
+
+
+def swap_blocks(x, axis, split, join):
+    pieces = jnp.split(x, lax.axis_size(axis), axis=split)
+    arrived = lax.all_to_all(jnp.stack(pieces), axis, 0, 0)
+    return jnp.concatenate(arrived, axis=join)
 
 
 def fibre_gram(fibres):
@@ -26,7 +32,7 @@
 
 def on_device(fields, x_factor, running_r):
     full_y = running_r.shape[0]
-    exchanged = lax.all_to_all(fields, "gx", split_axis=2, concat_axis=0, tiled=True)
+    exchanged = swap_blocks(fields, "gx", 2, 0)
     projected = project_local(x_factor, exchanged)
     fibres = lax.all_to_all(projected, "gy", split_axis=2, concat_axis=1, tiled=True)
     gram_sum = fibre_gram(fibres)

time: 706 us -> 672 us (0.952)
  blocking collectives: 206 us -> 183 us
  local copies, waits for them, and re-layouts: 62.8 us -> 49.8 us
    all_to_all x1, blocking collectives: 114 us -> 91.3 us  [swap_blocks(): arrived = lax.all_to_all(jnp.stack(pieces), axis, 0, 0)]
    another operation x0 -> x2, local copies, waits for them, and re-layouts: none -> 12.9 us  [the longest x1 12.5 us: project_local(): block.reshape(full_x, middle * part_cells)]
    reshape x1 -> x0, local copies, waits for them, and re-layouts: 12.5 us -> none  [project_local(): block.reshape(full_x, middle * part_cells)]
    all_to_all x1, local copies, waits for them, and re-layouts: 15.4 us -> 8.03 us  [swap_blocks(): arrived = lax.all_to_all(jnp.stack(pieces), axis, 0, 0)]
where the time goes in v2:
time: 672 us; the launch traced here: 664 us
  waiting for transfers between devices  257 us (38%)
  blocking collectives  183 us (27%)
  other arithmetic  121 us (18%)
  local copies, waits for them, and re-layouts  49.8 us (7%)
  matrix products  34.6 us (5%)
  between operations  17.6 us (3%)
    psum x1, waiting for transfers between devices, fibre_gram(): return lax.psum(local_gram, ('gx', 'gy'))  257 us
    another operation x22, other arithmetic, on_device(): upper_r = jnp.linalg.cholesky(total).T  118 us
    all_to_all x1, blocking collectives, on_device(): lax.all_to_all(projected, 'gy', split_axis=2, concat_axis=1, tiled=True)  92.1 us
    all_to_all x1, blocking collectives, swap_blocks(): arrived = lax.all_to_all(jnp.stack(pieces), axis, 0, 0)  91.3 us
  transfers between devices with their start and end apart: 1, of which 1 were waited for; matrix products, arithmetic and copies ran while one was open for 0% of the time, Pallas kernels for 0%

profile of v2, /device:TPU:2, one launch (start us, length us, event | category | flops | bytes accessed | tf_op | source)
XLA Modules:
  0.0 663.8 jit_solution(7904213924808287970)
XLA Ops:
  6.5 1.4 bitcast_dynamic-update-slice_fusion.7
  7.9 2.2 bitcast_dynamic-update-slice_fusion.6
  12.7 91.3 %all_to_all.23 = bf16[8,84,21,192]{3,1,2,0:T(8,128)(2,1)} all-to-all(bf16[8,84,21,192]{3,1,2,0:T(8,128)(2,1)S(1)} %bitcast_dynamic-update-slice_fusion), channel_id=1, replica_groups=mesh['gx'=8,'gy'=32] {'gx'}, dimensions={0} | all-to-all | bytes 10838016 | tf_op jit(solution)/shard_map/all_to_all | solution.py:9
  104.0 8.0 %copy.19 = bf16[8,84,21,192]{3,2,1,0:T(8,128)(2,1)} copy(bf16[8,84,21,192]{3,1,2,0:T(8,128)(2,1)} %all_to_all.23) | data formatting | bytes 10838016 | tf_op jit(solution)/shard_map/all_to_all | solution.py:9
  112.1 12.5 %reshape_reshape.3 = bf16[672,4032]{1,0:T(8,128)(2,1)} reshape(bf16[8,84,21,192]{3,2,1,0:T(8,128)(2,1)} %copy.19) | data formatting | bytes 10838016 | tf_op jit(solution)/shard_map/reshape;reshape | solution.py:26
  124.6 6.5 fusion
  131.1 4.5 copy.20
  135.6 3.7 copy.21
  139.4 92.1 %all_to_all.24 = bf16[336,21,192]{0,1,2:T(8,128)(2,1)S(1)} all-to-all(bf16[336,21,192]{0,1,2:T(8,128)(2,1)S(1)} %copy.21), channel_id=1, replica_groups=mesh['gx'=8,'gy'=32] {'gy'}, dimensions={2} | all-to-all | bytes 5419008 | tf_op jit(solution)/shard_map/all_to_all | solution.py:37
  231.5 2.2 copy.22
  233.7 6.0 all_to_all.20
  239.7 6.8 %convolution_bitcast_fusion = f32[672,672]{0,1:T(8,128)} fusion(bf16[336,672,6]{0,1,2:T(8,128)(2,1)} %all_to_all.20), kind=kOutput, calls=%fused_computation.4 | convolution fusion | flops 1820786688 | bytes 4515840 | tf_op jit(solution)/shard_map/dot_general | solution.py:14
  246.5 257.3 %all-reduce.3.cloned.1.call-done = f32[672,672]{0,1:T(8,128)} async-done(((f32[672,672]{0,1:T(8,128)}), f32[672,672]{0,1:T(8,128)}) %all-reduce.3.cloned.1.call-update) | async-done | bytes 1806352 | tf_op jit(solution)/shard_map/psum | solution.py:17
  503.9 8.2 %convolution_add_fusion = f32[672,672]{0,1:T(8,128)} fusion(f32[672,672]{0,1:T(8,128)} %all-reduce.3.cloned.1.call-done, f32[672,672]{1,0:T(8,128)S(1)} %copy-done), kind=kOutput, calls=%fused_computation.5 | convolution fusion | flops 3642024960 | bytes 5419008 | tf_op jit(solution)/shard_map/dot_general | solution.py:40
  512.1 3.1 copy.26
  515.3 2.5 fusion.1
  519.1 11.7 %cholesky.166 = f32[128,128]{1,0:T(8,128)S(1)} custom-call(f32[128,128]{1,0:T(8,128)S(1)} %cholesky.430), custom_call_target="Cholesky" | custom-call | tf_op jit(solution)/shard_map/jit(cholesky)/cholesky | solution.py:48
  530.8 9.8 %custom-call.43 = f32[1,128,128]{1,2,0:T(8,128)S(1)} custom-call(f32[1,128,128]{2,1,0:T(8,128)S(1)} %get-tuple-element.18), custom_call_target="InvertDiagBlocksLowerTriangular" | custom-call | tf_op jit(solution)/shard_map/jit(cholesky)/cholesky | solution.py:48
  540.6 1.4 cholesky.342
  542.1 2.1 constant_dynamic-update-slice_fusion.4
  545.5 11.7 %cholesky.189 = f32[128,128]{1,0:T(8,128)S(1)} custom-call(f32[128,128]{1,0:T(8,128)S(1)} %cholesky.434), custom_call_target="Cholesky" | custom-call | tf_op jit(solution)/shard_map/jit(cholesky)/cholesky | solution.py:48
  557.9 10.2 %custom-call.44 = f32[1,128,128]{1,2,0:T(8,128)S(1)} custom-call(f32[1,128,128]{2,1,0:T(8,128)S(1)} %get-tuple-element.15), custom_call_target="InvertDiagBlocksLowerTriangular" | custom-call | tf_op jit(solution)/shard_map/jit(cholesky)/cholesky | solution.py:48
  569.1 1.6 convolution_subtract_fusion.1
  570.7 11.7 %cholesky.356 = f32[128,128]{1,0:T(8,128)S(1)} custom-call(f32[128,128]{1,0:T(8,128)S(1)} %cholesky.439), custom_call_target="Cholesky" | custom-call | tf_op jit(solution)/shard_map/jit(cholesky)/cholesky | solution.py:48
  583.7 9.8 %custom-call.45 = f32[1,128,128]{1,2,0:T(8,128)S(1)} custom-call(f32[1,128,128]{2,1,0:T(8,128)S(1)} %get-tuple-element.12), custom_call_target="InvertDiagBlocksLowerTriangular" | custom-call | tf_op jit(solution)/shard_map/jit(cholesky)/cholesky | solution.py:48
  594.5 1.7 convolution_subtract_fusion.2
  596.2 11.8 %cholesky.375 = f32[128,128]{1,0:T(8,128)S(1)} custom-call(f32[128,128]{1,0:T(8,128)S(1)} %cholesky.444), custom_call_target="Cholesky" | custom-call | tf_op jit(solution)/shard_map/jit(cholesky)/cholesky | solution.py:48
  609.4 9.8 %custom-call.46 = f32[1,128,128]{1,2,0:T(8,128)S(1)} custom-call(f32[1,128,128]{2,1,0:T(8,128)S(1)} %get-tuple-element.9), custom_call_target="InvertDiagBlocksLowerTriangular" | custom-call | tf_op jit(solution)/shard_map/jit(cholesky)/cholesky | solution.py:48
  620.1 1.5 convolution_subtract_fusion.3
  621.6 11.7 %cholesky.394 = f32[128,128]{1,0:T(8,128)S(1)} custom-call(f32[128,128]{1,0:T(8,128)S(1)} %cholesky.449), custom_call_target="Cholesky" | custom-call | tf_op jit(solution)/shard_map/jit(cholesky)/cholesky | solution.py:48
  634.6 9.8 %custom-call.47 = f32[1,128,128]{1,2,0:T(8,128)S(1)} custom-call(f32[1,128,128]{2,1,0:T(8,128)S(1)} %get-tuple-element.6), custom_call_target="InvertDiagBlocksLowerTriangular" | custom-call | tf_op jit(solution)/shard_map/jit(cholesky)/cholesky | solution.py:48
  646.4 2.9 cholesky.415
  (40 shorter events, 18.4 us)
Async XLA Ops:
  6.5 497.3 %copy-start = (f32[672,672]{1,0:T(8,128)S(1)}, f32[672,672]{1,0:T(8,128)}, u32[]{:S(2)}) copy-start(f32[672,672]{1,0:T(8,128)} %param.5) | copy-start | bytes 5419012
  6.5 497.3 %all-reduce.3.cloned.1.call-start = ((), (), s32[]{:S(2)}) async-start(), calls=%async_computation.2 | async-start | bytes 4128768 | tf_op jit(solution)/shard_map/psum | solution.py:17
  6.5 4.8 copy-start.1
  112.1 12.5 %copy-start.3 = (bf16[672,336]{1,0:T(8,128)(2,1)S(1)}, bf16[672,336]{1,0:T(8,128)(2,1)}, u32[]{:S(2)}) copy-start(bf16[672,336]{1,0:T(8,128)(2,1)} %param.4) | copy-start | bytes 1354756
  517.7 1.3 copy-start.2
Sparse Core Ops, SparseCore 0:
  246.6 257.1 all-reduce.2
